TPU v7x, 32 devices: a whole 2x2x4 slice. The times are simulated.
32 devices in a mesh: gx: 4 (over y, x), gy: 2 (over core), gz: 4 (over z).
Axes of the slice: x: 2, y: 2, z: 4, core: 2. Of those that a mesh axis runs over, the one named last changes fastest.
Arguments:
- patches: bfloat16 [512, 6144], P(('gz', 'gx'), 'gy'), may hold values from -6 to 6
- modality: int32 [512], P(('gz', 'gx')), may hold values from 0 to 2
- gains: float32 [3, 6144], P(None, 'gy'), may hold values from 0.1 to 1.9
- biases: float32 [3, 6144], P(None, 'gy'), may hold values from -3 to 3
- weights: bfloat16 [3, 6144, 3072], P(None, ('gy', 'gz'), 'gx'), may hold values from -0.078125 to 0.078125
- segments: int32 [4, 128], P('gz'), may hold values from 0 to 3, never falling along the last dimension, each value on 1 to 64 neighbouring positions
- cotangent: bfloat16 [512, 3072], P(('gz', 'gy'), 'gx'), may hold values from -6 to 6
Outputs:
- attended: bfloat16 [512, 3072], P(('gz', 'gy'), 'gx')
- patch_gradient: float32 [512, 6144], P(('gz', 'gx'), 'gy')
Inputs may be any that keep to these rules, and one draw needn't show every extreme that they name: `segments`: within each pack the segment ids never fall, and each segment holds at most half of 128 patches.
All inputs are finite; a program needn't handle non-finite values.
Results may differ from a plain program's by a relative error of at most 0.02.
Values may be sent and summed in bfloat16 or wider, within the bound.
A program may use at most 64 MiB of HBM per device.

v0:
```python
import jax
import jax.numpy as jnp
from jax import lax
from jax.sharding import PartitionSpec as P

MODEL_WIDTH = 6144
HEAD_DIM = 128
EPS = 1e-06


def sum_over_width(totals):
    return lax.psum((totals[0], totals[1]), "gy")


def split_sum(partial_value):
    return lax.psum(partial_value, "gy").astype(jnp.float32)


def on_device(patches, modality, gains, biases, weights, segments, cotangent):
    values_f = patches.astype(jnp.float32)
    totals, squares = sum_over_width((jnp.sum(values_f, -1), jnp.sum(values_f * values_f, -1)))
    average = totals / MODEL_WIDTH
    variance = squares / MODEL_WIDTH - average * average
    mean_removed = values_f - average[:, None]
    inverse_deviation = lax.rsqrt(variance + EPS)[:, None]
    standardized_input = mean_removed * inverse_deviation
    levels = jnp.arange(gains.shape[0], dtype=jnp.int32)
    chosen = (modality[:, None] == levels[None, :])[:, :, None]
    gain_per_row = jnp.sum(jnp.where(chosen, gains[None], 0.0), 1)
    bias_per_row = jnp.sum(jnp.where(chosen, biases[None], 0.0), 1)
    layer_normalized = (standardized_input * gain_per_row + bias_per_row).astype(jnp.bfloat16)
    full_weights = lax.all_gather(weights, "gz", axis=1, tiled=True)
    partial_value = jnp.einsum(
        "rd,kdc->rkc",
        lax.all_gather(layer_normalized, "gx", axis=0, tiled=True),
        full_weights,
        preferred_element_type=jnp.float32,
    ).astype(jnp.bfloat16)
    pack_rows = partial_value.shape[0]
    own_rows = pack_rows // lax.axis_size("gy")
    offset = lax.axis_index("gy") * own_rows
    projected = split_sum(partial_value).astype(jnp.bfloat16)
    queries = lax.dynamic_slice_in_dim(projected[:, 0], offset, own_rows, 0)
    keys, values = (projected[:, 1], projected[:, 2])
    columns = full_weights.shape[2]
    head_count = columns // HEAD_DIM
    queries = queries.reshape(own_rows, head_count, HEAD_DIM)
    keys = keys.reshape(pack_rows, head_count, HEAD_DIM)
    values = values.reshape(pack_rows, head_count, HEAD_DIM)
    segment = segments[0]
    segment_query = lax.dynamic_slice_in_dim(segment, offset, own_rows, 0)
    allowed = (segment_query[:, None] == segment[None, :])[None]
    scaling = HEAD_DIM ** (-0.5)
    scores = jnp.einsum("qhd,khd->hqk", queries, keys, preferred_element_type=jnp.float32) * scaling
    exponent = jnp.where(allowed, jnp.exp(scores), 0.0)
    probs = exponent / jnp.sum(exponent, -1, keepdims=True)
    probs_b = probs.astype(jnp.bfloat16)
    attended = (
        jnp.einsum("hqk,khd->qhd", probs_b, values, preferred_element_type=jnp.float32)
        .astype(jnp.bfloat16)
        .reshape(own_rows, columns)
    )
    upstream = cotangent.reshape(own_rows, head_count, HEAD_DIM)
    dprobs = jnp.einsum("qhd,khd->hqk", upstream, values, preferred_element_type=jnp.float32)
    dvalues = jnp.einsum("hqk,qhd->khd", probs_b, upstream, preferred_element_type=jnp.float32)
    dscores = (probs * (dprobs - jnp.sum(probs * dprobs, -1, keepdims=True)) * scaling).astype(
        jnp.bfloat16
    )
    dqueries = jnp.einsum("hqk,khd->qhd", dscores, keys, preferred_element_type=jnp.float32)
    dkeys = jnp.einsum("hqk,qhd->khd", dscores, queries, preferred_element_type=jnp.float32)
    query_block = lax.dynamic_update_slice_in_dim(
        jnp.zeros((pack_rows, head_count, HEAD_DIM), jnp.float32), dqueries, offset, 0
    )
    stacked = (
        jnp.stack([query_block, dkeys, dvalues], 1)
        .reshape(pack_rows, 3, columns)
        .astype(jnp.bfloat16)
    )
    grad_proj = split_sum(stacked).astype(jnp.bfloat16)
    dnormed = lax.psum_scatter(
        jnp.einsum("rkc,kdc->rd", grad_proj, full_weights, preferred_element_type=jnp.float32),
        "gx",
        scatter_dimension=0,
        tiled=True,
    )
    normalized_gradient = dnormed * gain_per_row
    gradient_row_sum, weighted_row_sum = sum_over_width(
        (jnp.sum(normalized_gradient, -1), jnp.sum(normalized_gradient * standardized_input, -1))
    )
    patch_gradient = inverse_deviation * (
        normalized_gradient
        - gradient_row_sum[:, None] / MODEL_WIDTH
        - standardized_input * (weighted_row_sum[:, None] / MODEL_WIDTH)
    )
    return (attended, patch_gradient)


def solution(mesh):
    return jax.shard_map(
        on_device,
        mesh=mesh,
        in_specs=(
            P(("gz", "gx"), "gy"),
            P(("gz", "gx")),
            P(None, "gy"),
            P(None, "gy"),
            P(None, ("gy", "gz"), "gx"),
            P("gz", None),
            P(("gz", "gy"), "gx"),
        ),
        out_specs=(P(("gz", "gy"), "gx"), P(("gz", "gx"), "gy")),
        check_vma=False,
    )
```

profile of v0, /device:TPU:0, one launch (start us, length us, event | category | flops | bytes accessed | tf_op | source)
XLA Modules:
  0.0 362.8 jit_solution(14495759897900691260)
XLA Ops:
  7.3 0.7 all-gather.2.cloned.1.call-update
  8.0 0.1 copy-done.1
  8.1 0.2 convert_reduce_fusion
  8.3 2.6 all-reduce.1
  11.0 0.2 select_reduce_fusion.1
  11.2 0.1 fusion.14
  11.4 13.4 %all_gather.6 = bf16[128,3072]{1,0:T(8,128)(2,1)S(1)} all-gather(bf16[32,3072]{1,0:T(8,128)(2,1)S(1)} %fusion.14), channel_id=1, replica_groups=mesh['gx'=4,'gy'=2,'gz'=4] {'gx'}, dimensions={0}, use_global_device_ids=true | all-gather | bytes 983040 | tf_op jit(solution)/shard_map/all_gather | solution.py:35
  24.7 231.5 %all-gather.2.cloned.1.call-done = bf16[3,3072,768]{2,1,0:T(8,128)(2,1)} async-done(((bf16[3,768,768]{2,1,0:T(8,128)(2,1)}), bf16[3,3072,768]{2,1,0:T(8,128)(2,1)}) %all-gather.2.cloned.1.call-update) | async-done | bytes 14155792 | tf_op jit(solution)/shard_map/all_gather | solution.py:32
  256.3 7.9 %convolution_convert_fusion = bf16[128,3,768]{2,0,1:T(8,128)(2,1)} fusion(bf16[3,3072,768]{2,1,0:T(8,128)(2,1)} %all-gather.2.cloned.1.call-done, bf16[128,3072]{1,0:T(8,128)(2,1)S(1)} %all_gather.6), kind=kOutput, calls=%fused_computation.2 | convolution fusion | flops 1812234240 | bytes 15532032 | tf_op jit(solution)/shard_map/rd,kdc->rkc/dot_general | solution.py:33
  264.4 16.8 %all-reduce.5.cloned.1.call-done = bf16[128,3,768]{2,0,1:T(8,128)(2,1)} async-done(((bf16[128,3,768]{2,0,1:T(8,128)(2,1)}), bf16[128,3,768]{2,0,1:T(8,128)(2,1)}) %all-reduce.5.cloned.1.call-update) | async-done | bytes 589840 | tf_op jit(solution)/shard_map/psum | solution.py:16
  281.2 1.2 fusion.40
  282.5 0.2 copy.34
  282.7 0.2 copy.33
  282.8 0.3 fusion.26
  283.1 0.3 convolution_convert_fusion.1
  283.4 0.2 convolution_bitcast_fusion.1
  283.6 0.3 convolution_bitcast_fusion.2
  283.9 0.3 convolution_convert_fusion.2
  284.2 0.1 copy.47
  284.4 0.1 copy.46
  284.5 0.2 copy.42
  284.7 1.3 dynamic_update_slice.4
  286.1 0.1 copy.45
  286.2 0.9 pad_maximum_fusion
  287.2 21.1 %all-reduce.7.cloned.1.call-done = bf16[128,3,768]{2,0,1:T(8,128)(2,1)} async-done(((bf16[128,3,768]{2,0,1:T(8,128)(2,1)}), bf16[128,3,768]{2,0,1:T(8,128)(2,1)}) %all-reduce.7.cloned.1.call-update) | async-done | bytes 589840 | tf_op jit(solution)/shard_map/psum | solution.py:16
  308.2 10.9 %convolution_bitcast_fusion = f32[128,3072]{1,0:T(8,128)} fusion(bf16[128,3,768]{2,0,1:T(8,128)(2,1)} %all-reduce.7.cloned.1.call-done, bf16[3,3072,768]{2,1,0:T(8,128)(2,1)} %all-gather.2.cloned.1.call-done), kind=kOutput, calls=%fused_computation.1 | convolution fusion | flops 1811939328 | bytes 16318464 | tf_op jit(solution)/shard_map/rkc,kdc->rd/dot_general | solution.py:81
  319.2 0.2 fusion.7
  319.4 0.7 copy.69
  320.1 31.6 %reduce-scatter.2.cloned.1.call-done = f32[32,3072]{1,0:T(8,128)} async-done(((f32[128,3072]{1,0:T(8,128)}), f32[32,3072]{1,0:T(8,128)}) %reduce-scatter.2.cloned.1.call-update) | async-done | bytes 393232 | tf_op jit(solution)/shard_map/reduce_scatter | solution.py:80
  351.7 1.2 fusion.39
  352.9 2.5 all-reduce
  355.4 0.9 fusion.17
  (26 shorter events, 0.6 us)
Async XLA Ops:
  7.2 276.0 %copy-start = (bf16[64,768]{1,0:T(8,128)(2,1)S(1)}, bf16[64,768]{1,0:T(8,128)(2,1)}, u32[]{:S(2)}) copy-start(bf16[64,768]{1,0:T(8,128)(2,1)} %param.13) | copy-start | bytes 294916
  7.2 1.0 copy-start.1
  7.2 3.7 %copy-start.5 = (s32[32]{0:T(128)S(1)}, s32[32]{0:T(128)}, u32[]{:S(2)}) copy-start(s32[32]{0:T(128)} %param.8) | copy-start | bytes 388
  7.2 3.7 %copy-start.3 = (f32[3,3072]{1,0:T(4,128)S(1)}, f32[3,3072]{1,0:T(4,128)}, u32[]{:S(2)}) copy-start(f32[3,3072]{1,0:T(4,128)} %param.10) | copy-start | bytes 110596
  7.2 3.7 %copy-start.2 = (f32[3,3072]{1,0:T(4,128)S(1)}, f32[3,3072]{1,0:T(4,128)}, u32[]{:S(2)}) copy-start(f32[3,3072]{1,0:T(4,128)} %param.9) | copy-start | bytes 110596
  7.2 249.0 %all-gather.2.cloned.1.call-start = ((), (), s32[]{:S(2)}) async-start(), calls=%async_computation.1 | async-start | bytes 17694720 | tf_op jit(solution)/shard_map/all_gather | solution.py:32
  8.0 273.2 %all-reduce.5.cloned.1.call-start = ((), (), s32[]{:S(2)}) async-start(), calls=%async_computation.2 | async-start | bytes 1179648 | tf_op jit(solution)/shard_map/psum | solution.py:16
  24.7 239.4 %copy-start.4 = (s32[1,128]{1,0:T(1,128)S(1)}, s32[1,128]{1,0:T(1,128)}, u32[]{:S(2)}) copy-start(s32[1,128]{1,0:T(1,128)} %param.12) | copy-start | bytes 1540
  264.1 44.1 %all-reduce.7.cloned.1.call-start = ((), (), s32[]{:S(2)}) async-start(), calls=%async_computation.3 | async-start | bytes 1179648 | tf_op jit(solution)/shard_map/psum | solution.py:16
  287.1 64.6 %reduce-scatter.2.cloned.1.call-start = ((), (), s32[]{:S(2)}) async-start(), calls=%async_computation.4 | async-start | bytes 1966080 | tf_op jit(solution)/shard_map/reduce_scatter | solution.py:80
Sparse Core Ops, SparseCore 0:
  9.6 246.6 all-gather.1
  264.3 16.8 all-reduce.4
  287.2 20.9 all-reduce.6
  319.3 32.3 reduce-scatter.1
where the time goes:
time: 363 us
  waiting for transfers between devices  302 us (83%)
  matrix products  20.3 us (6%)
  blocking collectives  18.5 us (5%)
  between operations  14 us (4%)
  local copies, waits for them, and re-layouts  4.51 us (1%)
  other arithmetic  3.66 us (1%)
    all_gather x1, waiting for transfers between devices, on_device(): full_weights = lax.all_gather(weights, 'gz', axis=1, tiled=True)  232 us
    psum x2, waiting for transfers between devices, split_sum(): return lax.psum(partial_value, 'gy').astype(jnp.float32)  37.9 us
    reduce_scatter x1, waiting for transfers between devices, on_device(): lax.psum_scatter(jnp.einsum('rkc,kdc->rd', grad_proj, full_weights, prefe...  31.6 us
    all_gather x1, blocking collectives, on_device(): lax.all_gather(layer_normalized, 'gx', axis=0, tiled=True)  13.4 us
    dot_general x1, matrix products, on_device(): jnp.einsum('rkc,kdc->rd', grad_proj, full_weights, preferred_element_type...  10.9 us
    dot_general x1, matrix products, on_device(): jnp.einsum('rd,kdc->rkc', lax.all_gather(layer_normalized, 'gx', axis=0,...  7.86 us
  transfers between devices with their start and end apart: 4, of which 4 were waited for; matrix products, arithmetic and copies ran while one was open for 0% of the time, Pallas kernels for 0%

commit v1 on v0

--- a/solution.py
+++ b/solution.py
@@ -8,12 +8,17 @@
 EPS = 1e-06
 
 
+def gather_and_add(x, name):
+    shards = lax.all_gather(x, name)
+    return jnp.sum(shards, axis=0)
+
+
 def sum_over_width(totals):
     return lax.psum((totals[0], totals[1]), "gy")
 
 
 def split_sum(partial_value):
-    return lax.psum(partial_value, "gy").astype(jnp.float32)
+    return gather_and_add(partial_value, "gy").astype(jnp.float32)
 
 
 def on_device(patches, modality, gains, biases, weights, segments, cotangent):

time: 363 us -> 346 us (0.953)
  waiting for transfers between devices: 302 us -> 283 us
    psum x2 -> x0, waiting for transfers between devices: 37.9 us -> none  [split_sum(): return lax.psum(partial_value, 'gy').astype(jnp.float32)]
    all_gather x0 -> x2, waiting for transfers between devices: none -> 19 us  [gather_and_add(): shards = lax.all_gather(x, name)]
where the time goes in v1:
time: 346 us; the launch traced here: 345 us
  waiting for transfers between devices  283 us (82%)
  matrix products  20.1 us (6%)
  blocking collectives  18.5 us (5%)
  between operations  14 us (4%)
  other arithmetic  5.88 us (2%)
  local copies, waits for them, and re-layouts  4.03 us (1%)
    all_gather x1, waiting for transfers between devices, on_device(): full_weights = lax.all_gather(weights, 'gz', axis=1, tiled=True)  232 us
    reduce_scatter x1, waiting for transfers between devices, on_device(): lax.psum_scatter(jnp.einsum('rkc,kdc->rd', grad_proj, full_weights, prefe...  31.6 us
    all_gather x2, waiting for transfers between devices, gather_and_add(): shards = lax.all_gather(x, name)  19 us
    all_gather x1, blocking collectives, on_device(): lax.all_gather(layer_normalized, 'gx', axis=0, tiled=True)  13.4 us
    dot_general x1, matrix products, on_device(): jnp.einsum('rkc,kdc->rd', grad_proj, full_weights, preferred_element_type...  10.7 us
    dot_general x1, matrix products, on_device(): jnp.einsum('rd,kdc->rkc', lax.all_gather(layer_normalized, 'gx', axis=0,...  7.86 us
  transfers between devices with their start and end apart: 4, of which 4 were waited for; matrix products, arithmetic and copies ran while one was open for 0% of the time, Pallas kernels for 0%

profile of v1, /device:TPU:0, one launch (start us, length us, event | category | flops | bytes accessed | tf_op | source)
XLA Modules:
  0.0 345.4 jit_solution(2215020896399271148)
XLA Ops:
  7.3 0.7 all-gather.5.cloned.1.call-update
  8.0 0.1 copy-done.1
  8.1 0.2 convert_reduce_fusion
  8.3 2.6 all-reduce.1
  11.0 0.2 select_reduce_fusion.1
  11.2 0.1 fusion.14
  11.4 13.4 %all_gather.16 = bf16[128,3072]{1,0:T(8,128)(2,1)S(1)} all-gather(bf16[32,3072]{1,0:T(8,128)(2,1)S(1)} %fusion.14), channel_id=1, replica_groups=mesh['gx'=4,'gy'=2,'gz'=4] {'gx'}, dimensions={0}, use_global_device_ids=true | all-gather | bytes 983040 | tf_op jit(solution)/shard_map/all_gather | solution.py:40
  24.7 231.5 %all-gather.5.cloned.1.call-done = bf16[3,3072,768]{2,1,0:T(8,128)(2,1)} async-done(((bf16[3,768,768]{2,1,0:T(8,128)(2,1)}), bf16[3,3072,768]{2,1,0:T(8,128)(2,1)}) %all-gather.5.cloned.1.call-update) | async-done | bytes 14155792 | tf_op jit(solution)/shard_map/all_gather | solution.py:37
  256.3 7.9 %convolution_convert_fusion = bf16[128,3,768]{2,0,1:T(8,128)(2,1)} fusion(bf16[3,3072,768]{2,1,0:T(8,128)(2,1)} %all-gather.5.cloned.1.call-done, bf16[128,3072]{1,0:T(8,128)(2,1)S(1)} %all_gather.16), kind=kOutput, calls=%fused_computation.2 | convolution fusion | flops 1812234240 | bytes 15532032 | tf_op jit(solution)/shard_map/rd,kdc->rkc/dot_general | solution.py:38
  264.3 0.1 broadcast_compare_fusion
  264.4 7.3 %all-gather.9.cloned.1.call-done = bf16[256,3,768]{2,0,1:T(8,128)(2,1)} async-done(((bf16[128,3,768]{2,0,1:T(8,128)(2,1)}), bf16[256,3,768]{2,0,1:T(8,128)(2,1)}) %all-gather.9.cloned.1.call-update) | async-done | bytes 1179664 | tf_op jit(solution)/shard_map/all_gather | solution.py:12
  271.7 1.5 reduce_sum.100
  273.3 0.1 reshape.134
  273.4 0.2 copy.38
  273.6 0.2 copy.37
  273.8 0.3 fusion.26
  274.1 0.3 convolution_convert_fusion.1
  274.3 0.2 convolution_bitcast_fusion.1
  274.5 0.3 convolution_bitcast_fusion.2
  274.8 0.3 convolution_convert_fusion.2
  275.2 0.2 copy.46
  275.4 1.3 dynamic_update_slice.4
  276.8 1.1 copy.49
  277.9 11.6 %all-gather.7.cloned.1.call-done = bf16[2,128,3,768]{3,1,2,0:T(8,128)(2,1)} async-done(((bf16[1,128,3,768]{3,1,2,0:T(8,128)(2,1)}), bf16[2,128,3,768]{3,1,2,0:T(8,128)(2,1)}) %all-gather.7.cloned.1.call-update) | async-done | bytes 1179664 | tf_op jit(solution)/shard_map/all_gather | solution.py:12
  289.5 1.5 reduce_sum.103
  291.0 10.7 %convolution_bitcast_fusion = f32[128,3072]{1,0:T(8,128)} fusion(bf16[128,3,768]{2,0,1:T(8,128)(2,1)S(1)} %reduce_sum.103, bf16[3,3072,768]{2,1,0:T(8,128)(2,1)} %all-gather.5.cloned.1.call-done), kind=kOutput, calls=%fused_computation.1 | convolution fusion | flops 1811939328 | bytes 16318464 | tf_op jit(solution)/shard_map/rkc,kdc->rd/dot_general | solution.py:86
  301.8 0.2 fusion.7
  302.0 0.7 copy.75
  302.7 31.6 %reduce-scatter.2.cloned.1.call-done = f32[32,3072]{1,0:T(8,128)} async-done(((f32[128,3072]{1,0:T(8,128)}), f32[32,3072]{1,0:T(8,128)}) %reduce-scatter.2.cloned.1.call-update) | async-done | bytes 393232 | tf_op jit(solution)/shard_map/reduce_scatter | solution.py:85
  334.3 1.2 fusion.39
  335.5 2.5 all-reduce
  338.0 0.9 fusion.17
  (26 shorter events, 0.5 us)
Async XLA Ops:
  7.2 266.9 %copy-start = (bf16[64,768]{1,0:T(8,128)(2,1)S(1)}, bf16[64,768]{1,0:T(8,128)(2,1)}, u32[]{:S(2)}) copy-start(bf16[64,768]{1,0:T(8,128)(2,1)} %param.13) | copy-start | bytes 294916
  7.2 1.0 copy-start.1
  7.2 3.7 %copy-start.5 = (s32[32]{0:T(128)S(1)}, s32[32]{0:T(128)}, u32[]{:S(2)}) copy-start(s32[32]{0:T(128)} %param.8) | copy-start | bytes 388
  7.2 3.7 %copy-start.3 = (f32[3,3072]{1,0:T(4,128)S(1)}, f32[3,3072]{1,0:T(4,128)}, u32[]{:S(2)}) copy-start(f32[3,3072]{1,0:T(4,128)} %param.10) | copy-start | bytes 110596
  7.2 3.7 %copy-start.2 = (f32[3,3072]{1,0:T(4,128)S(1)}, f32[3,3072]{1,0:T(4,128)}, u32[]{:S(2)}) copy-start(f32[3,3072]{1,0:T(4,128)} %param.9) | copy-start | bytes 110596
  7.2 249.0 %all-gather.5.cloned.1.call-start = ((), (), s32[]{:S(2)}) async-start(), calls=%async_computation.1 | async-start | bytes 17694720 | tf_op jit(solution)/shard_map/all_gather | solution.py:37
  8.0 263.7 %all-gather.9.cloned.1.call-start = ((), (), s32[]{:S(2)}) async-start(), calls=%async_computation.4 | async-start | bytes 1769472 | tf_op jit(solution)/shard_map/all_gather | solution.py:12
  24.7 239.4 %copy-start.4 = (s32[1,128]{1,0:T(1,128)S(1)}, s32[1,128]{1,0:T(1,128)}, u32[]{:S(2)}) copy-start(s32[1,128]{1,0:T(1,128)} %param.12) | copy-start | bytes 1540
  264.1 25.4 %all-gather.7.cloned.1.call-start = ((), (), s32[]{:S(2)}) async-start(), calls=%async_computation.2 | async-start | bytes 1769472 | tf_op jit(solution)/shard_map/all_gather | solution.py:12
  277.9 56.4 %reduce-scatter.2.cloned.1.call-start = ((), (), s32[]{:S(2)}) async-start(), calls=%async_computation.3 | async-start | bytes 1966080 | tf_op jit(solution)/shard_map/reduce_scatter | solution.py:85
Sparse Core Ops, SparseCore 0:
  9.6 246.6 all-gather.4
  264.3 7.3 all-gather.8
  278.0 11.4 all-gather.6
  301.9 32.3 reduce-scatter.1
